TPU v7x, 32 devices: a whole 2x2x4 slice. The times are simulated.
32 devices in a mesh: row: 4 (over z), col: 8 (over y, x, core).
Axes of the slice: x: 2, y: 2, z: 4, core: 2. Of those that a mesh axis runs over, the one named last changes fastest.
Arguments:
- diag_factor: float32 [512, 512], P('row', 'col'), as said below
- panel_factor: float32 [8192, 512], P('row', 'col'), may hold values from -0.0625 to 0.0625
- row_factor: float32 [512, 3072], P('row', 'col'), may hold values from -0.25 to 0.25
- trailing_factor: float32 [8192, 3072], P('row', 'col'), may hold values from -0.0625 to 0.0625
- panel_grad: float32 [8192, 512], P('row', 'col'), may hold values from -6 to 6
- diag_grad: float32 [512, 512], P('row', 'col'), may hold values from -6 to 6
- row_grad: float32 [512, 3072], P('row', 'col'), may hold values from -6 to 6
- trailing_grad: float32 [8192, 3072], P('row', 'col'), may hold values from -6 to 6
Outputs:
- panel_adjoint: float32 [8192, 512], P('row', 'col')
- trailing_out: float32 [8192, 3072], P('row', 'col')
- row_out: float32 [512, 3072], P('row', 'col')
- diag_out: float32 [512, 512], P('row', 'col')
Inputs may be any that keep to these rules, and one draw needn't show every extreme that they name: diag_factor is zero above its diagonal; its diagonal entries lie between 1 and 2.
All inputs are finite; a program needn't handle non-finite values.
Results may differ from a plain program's by a relative error of at most 0.00011.
Values sent between devices are 32-bit elements; how exact they have to be, the bound alone decides.
A program may use at most 64 MiB of HBM per device.

v0:
```python
import jax
import jax.numpy as jnp
from jax import lax
from jax.sharding import PartitionSpec as P


def on_device(
    diag_factor,
    panel_factor,
    row_factor,
    trailing_factor,
    panel_grad,
    diag_grad,
    row_grad,
    trailing_grad,
):
    high = lax.Precision.HIGHEST
    tile_rows = lax.all_gather(diag_factor, "row", axis=0, tiled=True)
    whole_diag = lax.all_gather(tile_rows, "col", axis=1, tiled=True)
    width = panel_grad.shape[1]
    start_col = lax.axis_index("col") * width
    full_grad = lax.all_gather(panel_grad, "col", axis=1, tiled=True)
    solved = jax.scipy.linalg.solve_triangular(whole_diag, full_grad.T, lower=True, trans=1).T
    panel_adjoint = lax.dynamic_slice_in_dim(solved, start_col, width, 1)
    trailing_out = trailing_grad - jnp.dot(
        solved,
        lax.all_gather(row_factor, "row", axis=0, tiled=True),
        precision=high,
        preferred_element_type=jnp.float32,
    )
    contract = (((0,), (0,)), ((), ()))
    row_term = lax.dot_general(
        solved, trailing_factor, contract, precision=high, preferred_element_type=jnp.float32
    )
    diag_term = lax.dot_general(
        solved, panel_factor, contract, precision=high, preferred_element_type=jnp.float32
    )
    row_sum, diag_sum = (
        lax.psum_scatter(row_term, "row", scatter_dimension=0, tiled=True),
        lax.psum_scatter(diag_term, "row", scatter_dimension=0, tiled=True),
    )
    row_out = row_grad - row_sum
    height = diag_grad.shape[0]
    global_rows = lax.axis_index("row") * height + jnp.arange(height)[:, None]
    global_cols = start_col + jnp.arange(width)[None, :]
    diag_out = jnp.where(global_rows >= global_cols, diag_grad - diag_sum, jnp.float32(0.0))
    return (panel_adjoint, trailing_out, row_out, diag_out)


def solution(mesh):
    placed = (
        P("row", "col"),
        P("row", "col"),
        P("row", "col"),
        P("row", "col"),
        P("row", "col"),
        P("row", "col"),
        P("row", "col"),
        P("row", "col"),
    )
    return jax.shard_map(
        on_device,
        mesh=mesh,
        in_specs=placed,
        out_specs=(P("row", "col"), P("row", "col"), P("row", "col"), P("row", "col")),
        check_vma=False,
    )
```

profile of v0, /device:TPU:0, one launch (start us, length us, event | category | flops | bytes accessed | tf_op | source)
XLA Modules:
  0.0 176.6 jit_solution(3847113311811466690)
XLA Ops:
  7.2 0.0 copy-start
  7.2 0.0 all-gather.3.cloned.1.call-start
  7.2 17.2 %all_gather.12 = f32[512,64]{0,1:T(8,128)} all-gather(f32[128,64]{0,1:T(8,128)} %param.8), channel_id=1, replica_groups=mesh['row'=4,'col'=8] {'row'}, dimensions={0}, use_global_device_ids=true | all-gather | bytes 163840 | tf_op jit(solution)/shard_map/all_gather | solution.py:18
  24.4 0.0 all-gather.3.cloned.1.call-update
  24.4 0.0 all-gather.5.cloned.1.call-start
  24.5 0.7 all-gather.5.cloned.1.call-update
  25.2 0.0 reduce-scatter.5.cloned.1.call-start
  25.3 22.8 %all-gather.3.cloned.1.call-done = f32[512,512]{0,1:T(8,128)} async-done(((f32[512,64]{0,1:T(8,128)}), f32[512,512]{0,1:T(8,128)}) %all-gather.3.cloned.1.call-update) | async-done | bytes 1048592 | tf_op jit(solution)/shard_map/all_gather | solution.py:19
  48.1 2.3 %fusion.14 = f32[512,512]{0,1:T(8,128)} fusion(f32[512,512]{0,1:T(8,128)} %all-gather.3.cloned.1.call-done), kind=kLoop, calls=%fused_computation.19 | loop fusion | flops 524288 | bytes 2097152 | tf_op jit(solution)/shard_map/jit(_solve_triangular)/triangular_solve | solution.py:23
  50.4 14.1 %while.1 = (s32[]{:T(128)}, f32[512,512]{0,1:T(8,128)}, s32[4,2]{0,1:T(2,128)S(1)}, f32[4,128,128]{2,1,0:T(8,128)}, s32[]{:T(128)}) while((s32[]{:T(128)}, f32[512,512]{0,1:T(8,128)}, s32[4,2]{0,1:T(2,128)S(1)}, f32[4,128,128]{2,1,0:T(8,128)}, s32[]{:T(128)}) %tuple.24), condition=%wide.while_cond, body=%wide.while_body.sunk | while | flops 2 | bytes 393329 | solution.py:23
  50.4 0.1 constant_dynamic-slice_fusion.2
  50.5 0.5 fusion.34
  51.0 2.2 %dynamic-slice.12 = f32[128,128]{0,1:T(8,128)S(1)} dynamic-slice(f32[512,512]{0,1:T(8,128)} %get-tuple-element.66, s32[]{:T(128)} %bitcast.30, s32[]{:T(128)} %bitcast.31), dynamic_slice_sizes={128,128} | dynamic-slice | bytes 131076 | tf_op jit(solution)/shard_map/jit(_solve_triangular)/triangular_solve
  53.2 0.1 copy.16
  53.3 0.6 bitcast_dynamic-update-slice_fusion.2
  53.9 0.1 constant_dynamic-slice_fusion.2
  54.0 0.5 fusion.34
  54.5 2.2 %dynamic-slice.12 = f32[128,128]{0,1:T(8,128)S(1)} dynamic-slice(f32[512,512]{0,1:T(8,128)} %get-tuple-element.66, s32[]{:T(128)} %bitcast.30, s32[]{:T(128)} %bitcast.31), dynamic_slice_sizes={128,128} | dynamic-slice | bytes 131076 | tf_op jit(solution)/shard_map/jit(_solve_triangular)/triangular_solve
  56.8 0.1 copy.16
  56.9 0.6 bitcast_dynamic-update-slice_fusion.2
  57.5 0.1 constant_dynamic-slice_fusion.2
  57.6 0.5 fusion.34
  58.1 2.2 %dynamic-slice.12 = f32[128,128]{0,1:T(8,128)S(1)} dynamic-slice(f32[512,512]{0,1:T(8,128)} %get-tuple-element.66, s32[]{:T(128)} %bitcast.30, s32[]{:T(128)} %bitcast.31), dynamic_slice_sizes={128,128} | dynamic-slice | bytes 131076 | tf_op jit(solution)/shard_map/jit(_solve_triangular)/triangular_solve
  60.3 0.1 copy.16
  60.4 0.6 bitcast_dynamic-update-slice_fusion.2
  61.0 0.1 constant_dynamic-slice_fusion.2
  61.1 0.5 fusion.34
  61.6 2.1 %dynamic-slice.12 = f32[128,128]{0,1:T(8,128)S(1)} dynamic-slice(f32[512,512]{0,1:T(8,128)} %get-tuple-element.66, s32[]{:T(128)} %bitcast.30, s32[]{:T(128)} %bitcast.31), dynamic_slice_sizes={128,128} | dynamic-slice | bytes 131076 | tf_op jit(solution)/shard_map/jit(_solve_triangular)/triangular_solve
  63.8 0.1 copy.16
  63.9 0.6 bitcast_dynamic-update-slice_fusion.2
  64.5 40.3 %custom-call.4 = f32[4,128,128]{1,2,0:T(8,128)S(1)} custom-call(f32[4,128,128]{2,1,0:T(8,128)} %get-tuple-element.11), custom_call_target="InvertDiagBlocksLowerTriangular" | custom-call | tf_op jit(solution)/shard_map/jit(_solve_triangular)/triangular_solve | solution.py:23
  104.8 0.0 all-gather.5.cloned.1.call-done
  104.8 0.0 copy-start.9
  104.9 2.4 %fusion.12 = f32[128,2048]{1,0:T(8,128)S(1)} fusion(f32[512,2048]{1,0:T(8,128)} %bitcast.32, f32[4,128,128]{1,2,0:T(8,128)S(1)} %custom-call.4), kind=kOutput, calls=%fused_computation.16 | convolution fusion | flops 402653184 | bytes 2162688 | tf_op jit(solution)/shard_map/jit(_solve_triangular)/triangular_solve | solution.py:23
  107.2 0.0 copy-start.1
  107.2 2.7 %convolution_subtract_fusion.2 = f32[128,2048]{1,0:T(8,128)S(1)} fusion(f32[128,2048]{1,0:T(8,128)S(1)} %fusion.12, f32[512,2048]{1,0:T(8,128)} %bitcast.33, f32[512,512]{0,1:T(8,128)} %get-tuple-element.75), kind=kOutput, calls=%fused_computation.12 | convolution fusion | flops 402915328 | bytes 3211264 | tf_op jit(solution)/shard_map/jit(_solve_triangular)/triangular_solve | solution.py:23
  109.9 1.0 fusion.18
  110.9 0.0 copy-done.9
  110.9 0.0 copy-start.3
  110.9 2.3 %convolution_subtract_fusion.1 = f32[128,2048]{1,0:T(8,128)S(1)} fusion(f32[128,2048]{1,0:T(8,128)S(1)} %fusion.12, f32[128,2048]{1,0:T(8,128)S(1)} %fusion.18, f32[512,2048]{1,0:T(8,128)S(1)} %bitcast.34, f32[512,512]{0,1:T(8,128)} %get-tuple-element.75), kind=kOutput, calls=%fused_computation.11 | convolution fusion | flops 806092800 | bytes 4325376 | tf_op jit(solution)/shard_map/jit(_solve_triangular)/triangular_solve | solution.py:23
  113.3 1.0 fusion.19
  114.3 0.0 copy-start.5
  114.3 0.0 copy-start.14
  114.3 3.3 %fusion.6 = f32[128,2048]{1,0:T(8,128)S(1)} fusion(f32[128,2048]{1,0:T(8,128)S(1)} %fusion.12, f32[128,2048]{1,0:T(8,128)S(1)} %fusion.18, f32[128,2048]{1,0:T(8,128)S(1)} %fusion.19, f32[512,2048]{1,0:T(8,128)S(1)} %bitcast.35, f32[512,512]{0,1:T(8,128)} %get-tuple-element.75), kind=kOutput, calls=%fused_computation.10 | convolution fusion | flops 1209794560 | bytes 5439488 | tf_op jit(solution)/shard_map/jit(_solve_triangular)/triangular_solve | solution.py:23
  117.6 1.0 fusion.20
  118.7 0.0 copy-start.7
  118.7 1.0 copy-done.7
  119.6 0.0 copy-done.14
  119.6 4.8 %fusion.23 = f32[512,64]{0,1:T(8,128)} fusion(f32[2048,64]{0,1:T(8,128)S(1)} %copy-done.14, f32[128,2048]{1,0:T(8,128)S(1)} %fusion.12, f32[128,2048]{1,0:T(8,128)S(1)} %fusion.18, f32[128,2048]{1,0:T(8,128)S(1)} %fusion.19, f32[128,2048]{1,0:T(8,128)S(1)} %fusion.20), kind=kOutput, calls=%fused_computation.37 | convolution fusion | flops 808452096 | bytes 4849664 | tf_op jit(solution)/shard_map/dot_general | solution.py:35
  124.5 0.0 reduce-scatter.5.cloned.1.call-update
  124.5 0.0 copy-start.12
  124.5 0.0 reduce-scatter.3.cloned.1.call-start
  124.6 9.5 %fusion.24 = f32[512,384]{1,0:T(8,128)} fusion(f32[2048,384]{1,0:T(8,128)S(1)} %copy-done, f32[128,2048]{1,0:T(8,128)} %copy-done.1, f32[128,2048]{1,0:T(8,128)} %copy-done.3, f32[128,2048]{1,0:T(8,128)} %copy-done.5, f32[128,2048]{1,0:T(8,128)} %copy-done.7), kind=kOutput, calls=%fused_computation.38 | convolution fusion | flops 4834983936 | bytes 8126464 | tf_op jit(solution)/shard_map/dot_general | solution.py:32
  134.1 0.0 reduce-scatter.3.cloned.1.call-update
  134.2 19.7 %all_gather.15 = f32[512,384]{1,0:T(8,128)S(1)} all-gather(f32[128,384]{1,0:T(8,128)S(1)} %copy-done.12), channel_id=1, replica_groups=mesh['row'=4,'col'=8] {'row'}, dimensions={0}, use_global_device_ids=true | all-gather | bytes 983040 | tf_op jit(solution)/shard_map/all_gather | solution.py:27
  153.9 0.0 copy-start.10
  153.9 2.8 %pad_maximum_fusion = f32[512,2048]{1,0:T(8,128)S(1)} fusion(f32[128,2048]{1,0:T(8,128)} %copy-done.1, f32[128,2048]{1,0:T(8,128)} %copy-done.3, f32[128,2048]{1,0:T(8,128)} %copy-done.5, f32[128,2048]{1,0:T(8,128)} %copy-done.7), kind=kLoop, calls=%fused_computation.2 | loop fusion | flops 3145728 | bytes 8388608 | tf_op jit(solution)/shard_map/jit(_solve_triangular)/triangular_solve | solution.py:23
  156.7 0.8 dynamic-slice_bitcast_fusion
  157.6 0.0 copy-done.8
  157.6 1.0 copy-done.10
  158.6 8.4 %convolution_subtract_fusion = f32[2048,384]{1,0:T(8,128)} fusion(f32[2048,384]{1,0:T(8,128)S(1)} %copy-done.10, f32[512,384]{1,0:T(8,128)S(1)} %all_gather.15, f32[128,2048]{1,0:T(8,128)S(1)} %copy-done.2, f32[128,2048]{1,0:T(8,128)S(1)} %copy-done.4, f32[128,2048]{1,0:T(8,128)S(1)} %copy-done.6, f32[128,2048]{1,0:T(8,128)S(1)} %copy-done.8), kind=kOutput, calls=%fused_computation.9 | convolution fusion | flops 4835770368 | bytes 11272192 | tf_op jit(solution)/shard_map/dot_general | solution.py:25
  167.0 1.4 subtract_select_fusion
  168.4 0.0 copy-done.11
  168.4 1.6 sub.10
  (22 shorter events, 0.0 us)
Async XLA Ops:
  7.2 117.4 %copy-start = (f32[2048,384]{1,0:T(8,128)S(1)}, f32[2048,384]{1,0:T(8,128)}, u32[]{:S(2)}) copy-start(f32[2048,384]{1,0:T(8,128)} %param.11) | copy-start | bytes 9437188
  7.2 40.9 %all-gather.3.cloned.1.call-start = ((), (), s32[]{:S(2)}) async-start(), calls=%async_computation.2 | async-start | bytes 1179648 | tf_op jit(solution)/shard_map/all_gather | solution.py:19
  24.4 80.4 %all-gather.5.cloned.1.call-start = ((), (), s32[]{:S(2)}) async-start(), calls=%async_computation.3 | async-start | bytes 4718592 | tf_op jit(solution)/shard_map/all_gather | solution.py:22
  25.2 141.8 %reduce-scatter.5.cloned.1.call-start = ((), (), s32[]{:S(2)}) async-start(), calls=%async_computation.5 | async-start | bytes 163840 | tf_op jit(solution)/shard_map/reduce_scatter | solution.py:40
  104.8 6.1 %copy-start.9 = (f32[2048,512]{0,1:T(8,128)S(1)}, f32[2048,512]{0,1:T(8,128)}, u32[]{:S(2)}) copy-start(f32[2048,512]{0,1:T(8,128)} %all-gather.5.cloned.1.call-done) | copy-start | bytes 12582916
  107.2 11.4 %copy-start.1 = (f32[128,2048]{1,0:T(8,128)}, f32[128,2048]{1,0:T(8,128)S(1)}, u32[]{:S(2)}) copy-start(f32[128,2048]{1,0:T(8,128)S(1)} %fusion.12) | copy-start | bytes 3145732
  110.9 7.7 %copy-start.3 = (f32[128,2048]{1,0:T(8,128)}, f32[128,2048]{1,0:T(8,128)S(1)}, u32[]{:S(2)}) copy-start(f32[128,2048]{1,0:T(8,128)S(1)} %fusion.18) | copy-start | bytes 3145732
  114.3 4.3 %copy-start.5 = (f32[128,2048]{1,0:T(8,128)}, f32[128,2048]{1,0:T(8,128)S(1)}, u32[]{:S(2)}) copy-start(f32[128,2048]{1,0:T(8,128)S(1)} %fusion.19) | copy-start | bytes 3145732
  114.3 5.3 %copy-start.14 = (f32[2048,64]{0,1:T(8,128)S(1)}, f32[2048,64]{0,1:T(8,128)}, u32[]{:S(2)}) copy-start(f32[2048,64]{0,1:T(8,128)} %param.9) | copy-start | bytes 1572868
  118.7 1.0 copy-start.7
  124.5 9.7 %copy-start.12 = (f32[128,384]{1,0:T(8,128)S(1)}, f32[128,384]{1,0:T(8,128)}, u32[]{:S(2)}) copy-start(f32[128,384]{1,0:T(8,128)} %param.10) | copy-start | bytes 589828
  124.5 43.9 %reduce-scatter.3.cloned.1.call-start = ((), (), s32[]{:S(2)}) async-start(), calls=%async_computation.4 | async-start | bytes 983040 | tf_op jit(solution)/shard_map/reduce_scatter | solution.py:39
  153.9 3.7 %copy-start.2 = (f32[128,2048]{1,0:T(8,128)S(1)}, f32[128,2048]{1,0:T(8,128)}, u32[]{:S(2)}) copy-start(f32[128,2048]{1,0:T(8,128)} %copy-done.1) | copy-start | bytes 3145732
  153.9 3.7 %copy-start.4 = (f32[128,2048]{1,0:T(8,128)S(1)}, f32[128,2048]{1,0:T(8,128)}, u32[]{:S(2)}) copy-start(f32[128,2048]{1,0:T(8,128)} %copy-done.3) | copy-start | bytes 3145732
  153.9 3.7 %copy-start.6 = (f32[128,2048]{1,0:T(8,128)S(1)}, f32[128,2048]{1,0:T(8,128)}, u32[]{:S(2)}) copy-start(f32[128,2048]{1,0:T(8,128)} %copy-done.5) | copy-start | bytes 3145732
  153.9 3.7 %copy-start.8 = (f32[128,2048]{1,0:T(8,128)S(1)}, f32[128,2048]{1,0:T(8,128)}, u32[]{:S(2)}) copy-start(f32[128,2048]{1,0:T(8,128)} %copy-done.7) | copy-start | bytes 3145732
  153.9 4.7 %copy-start.10 = (f32[2048,384]{1,0:T(8,128)S(1)}, f32[2048,384]{1,0:T(8,128)}, u32[]{:S(2)}) copy-start(f32[2048,384]{1,0:T(8,128)} %param.15) | copy-start | bytes 9437188
  158.6 8.4 %copy-start.13 = (f32[128,64]{0,1:T(8,128)S(1)}, f32[128,64]{0,1:T(8,128)}, u32[]{:S(2)}) copy-start(f32[128,64]{0,1:T(8,128)} %param.13) | copy-start | bytes 98308
  158.6 9.8 %copy-start.11 = (f32[128,384]{1,0:T(8,128)S(1)}, f32[128,384]{1,0:T(8,128)}, u32[]{:S(2)}) copy-start(f32[128,384]{1,0:T(8,128)} %param.14) | copy-start | bytes 589828
Sparse Core Ops, SparseCore 0:
  24.5 23.4 all-gather.2
  50.0 37.0 all-gather.4
  124.6 19.6 reduce-scatter.4
  146.5 21.3 reduce-scatter.2
where the time goes:
time: 177 us
  other arithmetic  48.5 us (27%)
  blocking collectives  36.9 us (21%)
  matrix products  36.5 us (21%)
  waiting for transfers between devices  23.6 us (13%)
  local copies, waits for them, and re-layouts  16.9 us (10%)
  between operations  14 us (8%)
    another operation x4, other arithmetic, on_device(): jax.scipy.linalg.solve_triangular(whole_diag, full_grad.T, lower=True, tr...  45.4 us
    all_gather x1, waiting for transfers between devices, on_device(): whole_diag = lax.all_gather(tile_rows, 'col', axis=1, tiled=True)  22.8 us
    all_gather x1, blocking collectives, on_device(): lax.all_gather(row_factor, 'row', axis=0, tiled=True)  19.7 us
    all_gather x1, blocking collectives, on_device(): tile_rows = lax.all_gather(diag_factor, 'row', axis=0, tiled=True)  17.2 us
    another operation x20, local copies, waits for them, and re-layouts  14.1 us
    another operation x7, matrix products, on_device(): jax.scipy.linalg.solve_triangular(whole_diag, full_grad.T, lower=True, tr...  13.7 us
    dot_general x1, matrix products, on_device(): lax.dot_general(solved, trailing_factor, contract, precision=high, prefer...  9.55 us
    dot_general x1, matrix products, on_device(): jnp.dot(solved, lax.all_gather(row_factor, 'row', axis=0, tiled=True), pr...  8.39 us
  transfers between devices with their start and end apart: 4, of which 1 were waited for; matrix products, arithmetic and copies ran while one was open for 45% of the time, Pallas kernels for 0%

commit v1 on v0

v1 whole, which is shorter than its diff:
```python
import functools
import math

import jax
import jax.numpy as jnp
from jax import lax
from jax.experimental import pallas as pl
from jax.experimental.pallas import tpu as pltpu
from jax.sharding import PartitionSpec as P

MESH = pl.DeviceIdType.MESH
F32 = jnp.float32
BF16 = jnp.bfloat16
CORES = 2


def split(x):
    hi = x.astype(BF16)
    return hi, (x - hi.astype(F32)).astype(BF16)


def dot3(a, b, dims=(((1,), (0,)), ((), ()))):
    dot = functools.partial(lax.dot_general, dimension_numbers=dims, preferred_element_type=F32)
    return dot(a[0], b[0]) + (dot(a[0], b[1]) + dot(a[1], b[0]))


def dot_high(a, b):
    return jnp.dot(a, b, precision=lax.Precision.HIGHEST, preferred_element_type=F32)


def iota(shape, dim):
    return lax.broadcasted_iota(jnp.int32, shape, dim)


def invert_base(a):
    n = a.shape[0]
    i, j = iota((n, n), 0), iota((n, n), 1)
    eye = i == j
    d = jnp.where(eye, a, 0.0)
    inv_col = 1.0 / jnp.sum(d, axis=1, keepdims=True)
    inv_row = 1.0 / jnp.sum(d, axis=0, keepdims=True)
    inv = jnp.where(eye, inv_col, 0.0)
    step = 1
    while step < n:
        pair = (i // (2 * step) == j // (2 * step)) & (i // step < j // step)
        part = jnp.where(pair, a, 0.0)
        if step == 1:
            inv = inv - part * inv_col * inv_row
        else:
            inv = inv - dot_high(dot_high(inv, part), inv)
        step *= 2
    return inv


class Gather:
    def __init__(self, place, side, buf, own, sems):
        self.z, self.y, self.x, self.core = place
        self.s, self.buf, self.own = side, buf, own
        self.p1s, self.p1r, self.p2s, self.p2r, self.cs, self.cr = sems

    def col(self, dy, dx, core):
        s = self.s
        return (lax.rem(self.y + dy + s, s) * s + lax.rem(self.x + dx + s, s)) * CORES + core

    def half(self, ref, half):
        rows = self.buf.shape[-2] // 2
        lead = (slice(None),) * (len(ref.shape) - 2)
        return ref.at[lead + (pl.ds(half * rows, rows), slice(None))]

    def block(self, dy, dx, core, half):
        return self.half(self.buf.at[self.col(dy, dx, core)], half)

    def source(self, dy, dx, half):
        if dy == 0 and dx == 0:
            return self.half(self.own, half)
        return self.block(dy, dx, self.core, half)

    def copy(self, dy, dx, half, send, recv, to):
        return pltpu.make_async_remote_copy(
            src_ref=self.source(dy, dx, half),
            dst_ref=self.block(dy, dx, self.core, half),
            send_sem=send,
            recv_sem=recv,
            device_id=(self.z, to),
            device_id_type=MESH,
        )

    def first(self, half, k):
        to = self.col(0, k, self.core) if half == 0 else self.col(k, 0, self.core)
        return self.copy(0, 0, half, self.p1s.at[half, k], self.p1r.at[half, k], to)

    def second(self, half, k, m):
        dy, dx = (0, -k) if half == 0 else (-k, 0)
        to = self.col(m, 0, self.core) if half == 0 else self.col(0, m, self.core)
        return self.copy(dy, dx, half, self.p2s.at[half, k, m], self.p2r.at[half, k, m], to)

    def across(self, dy, dx, half):
        at = dy * self.s + dx
        to = self.col(0, 0, 1 - self.core)
        return self.copy(-dy, -dx, half, self.cs.at[half, at], self.cr.at[half, at], to)

    def start_first(self):
        for k in range(1, self.s):
            for half in range(2):
                self.first(half, k).start()

    def start_own(self):
        for m in range(1, self.s):
            for half in range(2):
                self.second(half, 0, m).start()
        for half in range(2):
            self.across(0, 0, half).start()

    def relay(self):
        for k in range(1, self.s):
            for half in range(2):
                self.first(half, k).wait_recv()
                for m in range(1, self.s):
                    self.second(half, k, m).start()
                dy, dx = (0, k) if half == 0 else (k, 0)
                self.across(dy, dx, half).start()

    def pass_own(self):
        for m in range(1, self.s):
            for half in range(2):
                self.second(half, 0, m).wait_recv()
                dy, dx = (m, 0) if half == 0 else (0, m)
                self.across(dy, dx, half).start()

    def pass_relayed(self):
        for k in range(1, self.s):
            for m in range(1, self.s):
                for half in range(2):
                    self.second(half, k, m).wait_recv()
                    dy, dx = (m, k) if half == 0 else (k, m)
                    self.across(dy, dx, half).start()

    def wait_chip(self, dy, dx):
        for half in range(2):
            self.across(dy, dx, half).wait_recv()

    def wait_sends(self):
        s = self.s
        for half in range(2):
            for k in range(1, s):
                self.first(half, k).wait_send()
            for k in range(s):
                for m in range(1, s):
                    self.second(half, k, m).wait_send()
            for dy in range(s):
                for dx in range(s):
                    self.across(dy, dx, half).wait_send()


def kernel(
    nz, side, dt_hbm, gt_hbm, p_hbm, r_hbm, t_hbm, dg_hbm, rg_hbm, tg_hbm,
    pa_hbm, to_hbm, ro_hbm, do_hbm,
    dbuf, gbuf, rbuf, tbuf, pbuf, dgbuf, rgbuf, tgbuf, pabuf, dobuf,
    aup, inv_t, tp_hi, tp_lo, g_hi, g_lo, wbuf, ubuf, rsbuf,
    d_sems, g_sems, zs, zr, rs_s, rs_r, us, ur, local, outs,
):
    z = lax.axis_index("row")
    c = lax.axis_index("col")
    core = lax.rem(c, CORES)
    chip = c // CORES
    x, y = lax.rem(chip, side), chip // side
    place = (z, y, x, core)
    ncol, w, m = gbuf.shape
    n = ncol * w
    h = n // nz
    k = tbuf.shape[1]
    wide = tp_hi.shape[1]

    dgat = Gather(place, side, dbuf, dbuf.at[c], d_sems)
    ggat = Gather(place, side, gbuf, gt_hbm, g_sems)

    loads = [
        (dt_hbm, dbuf.at[c, z]),
        (t_hbm, tbuf),
        (p_hbm, pbuf),
        (gt_hbm, gbuf.at[c]),
        (r_hbm, rbuf.at[z]),
        (tg_hbm, tgbuf),
        (rg_hbm, rgbuf),
        (dg_hbm, dgbuf),
    ]
    loads = [pltpu.make_async_copy(a, b, local.at[i]) for i, (a, b) in enumerate(loads)]
    for load in loads:
        load.start()

    barrier = pltpu.get_barrier_semaphore()
    peers = [(lax.rem(z + i, nz), c) for i in range(1, nz)]
    peers += [(z, ggat.col(0, i, core)) for i in range(1, side)]
    peers += [(z, ggat.col(i, 0, core)) for i in range(1, side)]
    peers += [(z, ggat.col(0, 0, 1 - core))]
    for peer in peers:
        pl.semaphore_signal(barrier, inc=1, device_id=peer, device_id_type=MESH)
    pl.semaphore_wait(barrier, len(peers))

    def along_z(src, dst, send, recv, i):
        return pltpu.make_async_remote_copy(
            src_ref=src, dst_ref=dst, send_sem=send.at[i], recv_sem=recv.at[i],
            device_id=(lax.rem(z + i, nz), c), device_id_type=MESH,
        )

    d_z = [along_z(dt_hbm, dbuf.at[c, z], zs, zr, i) for i in range(1, nz)]
    r_z = [along_z(r_hbm, rbuf.at[z], rs_s, rs_r, i) for i in range(1, nz)]
    for copy in d_z:
        copy.start()
    ggat.start_first()
    for copy in r_z:
        copy.start()

    loads[0].wait()
    for copy in d_z:
        copy.wait_recv()
    dgat.start_first()
    dgat.start_own()

    for load in loads[1:]:
        load.wait()

    tile = 256

    def widen(i, carry):
        rows = pl.ds(pl.multiple_of(i * tile, tile), tile)
        hi, lo = split(tbuf[rows, :])
        tp_hi[rows, :k] = hi
        tp_lo[rows, :k] = lo
        tail = jnp.concatenate([pbuf[rows, :], jnp.zeros((tile, wide - k - w), F32)], axis=1)
        hi, lo = split(tail)
        tp_hi[rows, k:] = hi
        tp_lo[rows, k:] = lo
        return carry

    dgat.relay()
    ggat.start_own()
    ggat.relay()
    lax.fori_loop(0, m // tile, widen, 0)

    dgat.pass_own()
    dgat.pass_relayed()
    for dy in range(side):
        for dx in range(side):
            dgat.wait_chip(dy, dx)
    for col in range(ncol):
        aup[col * w:(col + 1) * w, :] = jnp.concatenate([dbuf[col, i] for i in range(nz)], axis=1)

    base = 128
    inv_t[...] = jnp.zeros((n, n), F32)
    for b in range(0, n, base):
        inv_t[b:b + base, b:b + base] = invert_base(aup[b:b + base, b:b + base])
    step = base
    while step < n:
        for b in range(0, n, 2 * step):
            up, low = slice(b, b + step), slice(b + step, b + 2 * step)
            inv_t[up, low] = -dot_high(dot_high(inv_t[up, up], aup[up, low]), inv_t[low, low])
        step *= 2

    def take(dy, dx):
        at = ggat.col(-dy, -dx, 0)
        rows = pl.ds(pl.multiple_of(at * w, CORES * w), CORES * w)
        value = split(gbuf[pl.ds(at, CORES)].reshape(CORES * w, m))
        g_hi[rows, :] = value[0]
        g_lo[rows, :] = value[1]
        wbuf[rows, :] = dot3(value, (tp_hi[...], tp_lo[...]))

    ggat.pass_own()
    ggat.wait_chip(0, 0)
    take(0, 0)
    for i in range(1, side):
        ggat.wait_chip(0, i)
        take(0, i)
        ggat.wait_chip(i, 0)
        take(i, 0)
    ggat.pass_relayed()
    for dy in range(1, side):
        for dx in range(1, side):
            ggat.wait_chip(dy, dx)
            take(dy, dx)

    wide_terms = split(wbuf[...])
    u_z = []
    for i in range(1, nz):
        to = lax.rem(z + i, nz)
        rows = pl.ds(pl.multiple_of(to * h, h), h)
        ubuf[rows, :] = dot3(split(inv_t[rows, :]), wide_terms)
        u_z.append(along_z(ubuf.at[rows], rsbuf.at[i], us, ur, i))
        if i > 1:
            u_z[i - 2].start()
    rows = pl.ds(pl.multiple_of(z * h, h), h)
    ubuf[rows, :] = dot3(split(inv_t[rows, :]), wide_terms)
    u_z[-1].start()

    for copy in r_z:
        copy.wait_recv()
    pick = (iota((n, wide - k), 0) == iota((n, wide - k), 1) + c * w) & (iota((n, wide - k), 1) < w)
    r_all = jnp.concatenate([rbuf[...].reshape(n, k), pick.astype(F32)], axis=1)
    both = split(dot3(split(inv_t[...].T), split(r_all)))
    wbuf_rows = (((0,), (0,)), ((), ()))

    def out_copies(i):
        rows = pl.ds(pl.multiple_of(i * tile, tile), tile)
        return (
            pltpu.make_async_copy(tgbuf.at[rows], to_hbm.at[rows], outs.at[0, i]),
            pltpu.make_async_copy(pabuf.at[rows], pa_hbm.at[rows], outs.at[1, i]),
        )

    tp_hi[:n, :] = both[0]
    tp_lo[:n, :] = both[1]

    def trail(i, carry):
        rows = pl.ds(pl.multiple_of(i * tile, tile), tile)
        value = dot3((g_hi[:, rows], g_lo[:, rows]), (tp_hi[:n, :], tp_lo[:n, :]), wbuf_rows)
        tgbuf[rows, :] = tgbuf[rows, :] - value[:, :k]
        pabuf[rows, :] = value[:, k:k + w]
        for copy in out_copies(i):
            copy.start()
        return carry

    lax.fori_loop(0, m // tile, trail, 0)

    for copy in u_z:
        copy.wait_recv()
    total = ubuf[rows, :]
    for i in range(1, nz):
        total = total + rsbuf[i]
    rgbuf[...] = rgbuf[...] - total[:, :k]
    keep = iota((h, w), 0) + z * h >= iota((h, w), 1) + c * w
    dobuf[...] = jnp.where(keep, dgbuf[...] - total[:, k:k + w], 0.0)
    last = [
        pltpu.make_async_copy(rgbuf, ro_hbm, local.at[0]),
        pltpu.make_async_copy(dobuf, do_hbm, local.at[1]),
    ]
    for copy in last:
        copy.start()

    for copy in d_z + r_z + u_z:
        copy.wait_send()
    dgat.wait_sends()
    ggat.wait_sends()

    def drain(i, carry):
        for copy in out_copies(i):
            copy.wait()
        return carry

    lax.fori_loop(0, m // tile, drain, 0)
    for copy in last:
        copy.wait()


def on_device(nz, side, diag_factor, panel_factor, row_factor, trailing_factor, panel_grad, diag_grad, row_grad, trailing_grad):
    m, w = panel_grad.shape
    h = diag_factor.shape[0]
    k = row_factor.shape[1]
    ncol = CORES * side * side
    n = ncol * w
    wide = -(-(k + w) // 128) * 128
    dma = pltpu.SemaphoreType.DMA
    gather_sems = [
        dma((2, side)), dma((2, side)), dma((2, side, side)), dma((2, side, side)),
        dma((2, side * side)), dma((2, side * side)),
    ]
    vmem = pltpu.VMEM
    any_spec = pl.BlockSpec(memory_space=pl.ANY)
    shape = jax.ShapeDtypeStruct
    return pl.pallas_call(
        functools.partial(kernel, nz, side),
        out_shape=(shape((m, w), F32), shape((m, k), F32), shape((h, k), F32), shape((h, w), F32)),
        in_specs=[any_spec] * 8,
        out_specs=(any_spec,) * 4,
        scratch_shapes=[
            vmem((ncol, nz, w, h), F32), vmem((ncol, w, m), F32), vmem((nz, h, k), F32),
            vmem((m, k), F32), vmem((m, w), F32), vmem((h, w), F32), vmem((h, k), F32),
            vmem((m, k), F32), vmem((m, w), F32), vmem((h, w), F32),
            vmem((n, n), F32), vmem((n, n), F32),
            vmem((m, wide), BF16), vmem((m, wide), BF16),
            vmem((n, m), BF16), vmem((n, m), BF16),
            vmem((n, wide), F32), vmem((n, wide), F32), vmem((nz, h, wide), F32),
            gather_sems, list(gather_sems),
            dma((nz,)), dma((nz,)), dma((nz,)), dma((nz,)), dma((nz,)), dma((nz,)),
            dma((8,)), dma((2, m // 256)),
        ],
        compiler_params=pltpu.CompilerParams(
            collective_id=0, has_side_effects=True, vmem_limit_bytes=64000 * 1024
        ),
        name="panel_step",
    )(diag_factor.T, panel_grad.T, panel_factor, row_factor, trailing_factor, diag_grad, row_grad, trailing_grad)


def solution(mesh):
    nz, ncol = mesh.shape["row"], mesh.shape["col"]
    side = math.isqrt(ncol // CORES)
    spec = P("row", "col")
    return jax.shard_map(
        functools.partial(on_device, nz, side),
        mesh=mesh,
        in_specs=(spec,) * 8,
        out_specs=(spec,) * 4,
        check_vma=False,
    )
```

time: 177 us -> 79.9 us (0.45)
  the two profiles are of different devices: /device:TPU:0 before, /device:TPU:25 now
where the time goes in v1:
time: 79.9 us; the launch traced here: 79.6 us
  Pallas kernels  66.8 us (84%)
  local copies, waits for them, and re-layouts  12.2 us (15%)
    pallas_call x1, Pallas kernels, on_device(): pl.pallas_call(functools.partial(kernel, nz, side), out_shape=(shape((m,...  66.8 us
    unnamed x6, local copies, waits for them, and re-layouts  8.31 us
    pallas_call x2, local copies, waits for them, and re-layouts, on_device(): pl.pallas_call(functools.partial(kernel, nz, side), out_shape=(shape((m,...  3.87 us

profile of v1, /device:TPU:25, one launch (start us, length us, event | category | flops | bytes accessed | tf_op | source)
XLA Modules:
  0.0 79.6 jit_solution(13712028226856671814)
XLA Ops:
  0.6 1.5 %copy.13.dg_hbm = f32[128,64]{1,0:T(8,128)} copy(f32[128,64]{0,1:T(8,128)} %param.13) | data formatting | bytes 65536 | tf_op args[5]
  2.1 2.4 %copy.12.p_hbm = f32[2048,64]{1,0:T(8,128)} copy(f32[2048,64]{0,1:T(8,128)} %param.9) | data formatting | bytes 1048576 | tf_op args[1]
  4.5 66.8 %panel_step.1 = (f32[2048,64]{1,0:T(8,128)}, f32[2048,384]{1,0:T(8,128)}, f32[128,384]{1,0:T(8,128)}, f32[128,64]{1,0:T(8,128)}) custom-call(f32[64,128]{1,0:T(8,128)} %bitcast.3, f32[64,2048]{1,0:T(8,128)} %bitcast.2, f32[2048,64]{1,0:T(8,128)} %copy.12.p_hbm, f32[128,384]{1,0:T(8,128)} %r_hbm.1, f32[2048,384]{1,0:T(8,128)} %t_hbm.1, ...), custom_call_target="tpu_custom_call" | custom-call | tf_op jit(solution)/shard_map/panel_step/pallas_call | solution.py:368
  71.2 2.3 %copy.14 = f32[2048,64]{0,1:T(8,128)} copy(f32[2048,64]{1,0:T(8,128)} %get-tuple-element.4) | data formatting | bytes 1048576 | tf_op jit(solution)/shard_map/panel_step/pallas_call | solution.py:368
  73.6 1.5 %copy.15 = f32[128,64]{0,1:T(8,128)} copy(f32[128,64]{1,0:T(8,128)} %get-tuple-element.7) | data formatting | bytes 65536 | tf_op jit(solution)/shard_map/panel_step/pallas_call | solution.py:368
  75.1 0.0 copy-start
  75.1 3.8 %copy.18 = f32[2048,384]{1,0:T(8,128)} copy(f32[2048,384]{1,0:T(8,128)} %get-tuple-element.13) | data formatting | bytes 6291456
  78.9 0.0 copy-done
  78.9 0.7 copy.19
Async XLA Ops:
  75.1 3.8 %copy-start = (f32[128,384]{1,0:T(8,128)S(1)}, f32[128,384]{1,0:T(8,128)}, u32[]{:S(2)}) copy-start(f32[128,384]{1,0:T(8,128)} %get-tuple-element.14) | copy-start | bytes 589828

commit v2 on v1

--- a/solution.py
+++ b/solution.py
@@ -12,6 +12,7 @@
 F32 = jnp.float32
 BF16 = jnp.bfloat16
 CORES = 2
+VMEM_KIB = 36000
 
 
 def split(x):
@@ -227,7 +228,7 @@
         hi, lo = split(tbuf[rows, :])
         tp_hi[rows, :k] = hi
         tp_lo[rows, :k] = lo
-        tail = jnp.concatenate([pbuf[rows, :], jnp.zeros((tile, wide - k - w), F32)], axis=1)
+        tail = jnp.concatenate([pbuf[:, rows].T, jnp.zeros((tile, wide - k - w), F32)], axis=1)
         hi, lo = split(tail)
         tp_hi[rows, k:] = hi
         tp_lo[rows, k:] = lo
@@ -303,7 +304,7 @@
         rows = pl.ds(pl.multiple_of(i * tile, tile), tile)
         return (
             pltpu.make_async_copy(tgbuf.at[rows], to_hbm.at[rows], outs.at[0, i]),
-            pltpu.make_async_copy(pabuf.at[rows], pa_hbm.at[rows], outs.at[1, i]),
+            pltpu.make_async_copy(pabuf.at[:, rows], pa_hbm.at[:, rows], outs.at[1, i]),
         )
 
     tp_hi[:n, :] = both[0]
@@ -313,7 +314,7 @@
         rows = pl.ds(pl.multiple_of(i * tile, tile), tile)
         value = dot3((g_hi[:, rows], g_lo[:, rows]), (tp_hi[:n, :], tp_lo[:n, :]), wbuf_rows)
         tgbuf[rows, :] = tgbuf[rows, :] - value[:, :k]
-        pabuf[rows, :] = value[:, k:k + w]
+        pabuf[:, rows] = value[:, k:k + w].T
         for copy in out_copies(i):
             copy.start()
         return carry
@@ -326,8 +327,8 @@
     for i in range(1, nz):
         total = total + rsbuf[i]
     rgbuf[...] = rgbuf[...] - total[:, :k]
-    keep = iota((h, w), 0) + z * h >= iota((h, w), 1) + c * w
-    dobuf[...] = jnp.where(keep, dgbuf[...] - total[:, k:k + w], 0.0)
+    keep = iota((w, h), 1) + z * h >= iota((w, h), 0) + c * w
+    dobuf[...] = jnp.where(keep, dgbuf[...] - total[:, k:k + w].T, 0.0)
     last = [
         pltpu.make_async_copy(rgbuf, ro_hbm, local.at[0]),
         pltpu.make_async_copy(dobuf, do_hbm, local.at[1]),
@@ -365,15 +366,19 @@
     vmem = pltpu.VMEM
     any_spec = pl.BlockSpec(memory_space=pl.ANY)
     shape = jax.ShapeDtypeStruct
-    return pl.pallas_call(
+    operands = (
+        diag_factor.T, panel_grad.T, panel_factor.T, row_factor,
+        trailing_factor, diag_grad.T, row_grad, trailing_grad,
+    )
+    pa, to, ro, do = pl.pallas_call(
         functools.partial(kernel, nz, side),
-        out_shape=(shape((m, w), F32), shape((m, k), F32), shape((h, k), F32), shape((h, w), F32)),
-        in_specs=[any_spec] * 8,
+        out_shape=(shape((w, m), F32), shape((m, k), F32), shape((h, k), F32), shape((w, h), F32)),
+        in_specs=[pl.BlockSpec(memory_space=pltpu.HBM)] * 8,
         out_specs=(any_spec,) * 4,
         scratch_shapes=[
             vmem((ncol, nz, w, h), F32), vmem((ncol, w, m), F32), vmem((nz, h, k), F32),
-            vmem((m, k), F32), vmem((m, w), F32), vmem((h, w), F32), vmem((h, k), F32),
-            vmem((m, k), F32), vmem((m, w), F32), vmem((h, w), F32),
+            vmem((m, k), F32), vmem((w, m), F32), vmem((w, h), F32), vmem((h, k), F32),
+            vmem((m, k), F32), vmem((w, m), F32), vmem((w, h), F32),
             vmem((n, n), F32), vmem((n, n), F32),
             vmem((m, wide), BF16), vmem((m, wide), BF16),
             vmem((n, m), BF16), vmem((n, m), BF16),
@@ -383,10 +388,11 @@
             dma((8,)), dma((2, m // 256)),
         ],
         compiler_params=pltpu.CompilerParams(
-            collective_id=0, has_side_effects=True, vmem_limit_bytes=64000 * 1024
+            collective_id=0, has_side_effects=True, vmem_limit_bytes=VMEM_KIB * 1024
         ),
         name="panel_step",
-    )(diag_factor.T, panel_grad.T, panel_factor, row_factor, trailing_factor, diag_grad, row_grad, trailing_grad)
+    )(*(pltpu.with_memory_space_constraint(v, pltpu.HBM) for v in operands))
+    return pa.T, to, ro, do.T
 
 
 def solution(mesh):

time: 79.9 us -> 71.2 us (0.89)
  local copies, waits for them, and re-layouts: 12.2 us -> 3.75 us
    unnamed x6 -> x4, local copies, waits for them, and re-layouts: 8.31 us -> 3.75 us
    pallas_call x2 -> x0, local copies, waits for them, and re-layouts: 3.87 us -> none  [on_device(): pl.pallas_call(functools.partial(kernel, nz, side), out_shape=(shape((m,...]
where the time goes in v2:
time: 71.2 us; the launch traced here: 71.1 us
  Pallas kernels  66.7 us (94%)
  local copies, waits for them, and re-layouts  3.75 us (5%)
    pallas_call x1, Pallas kernels, on_device(): pl.pallas_call(functools.partial(kernel, nz, side), out_shape=(shape((w,...  66.7 us
    unnamed x4, local copies, waits for them, and re-layouts  3.75 us

profile of v2, /device:TPU:25, one launch (start us, length us, event | category | flops | bytes accessed | tf_op | source)
XLA Modules:
  0.0 71.1 jit_solution(11172317101794092695)
XLA Ops:
  0.6 66.7 %panel_step.1 = (f32[64,2048]{1,0:T(8,128)S(1)}, f32[2048,384]{1,0:T(8,128)S(1)}, f32[128,384]{1,0:T(8,128)S(1)}, f32[64,128]{1,0:T(8,128)S(1)}) custom-call(f32[64,128]{1,0:T(8,128)} %bitcast.10, f32[64,2048]{1,0:T(8,128)} %bitcast.8, f32[64,2048]{1,0:T(8,128)} %bitcast.9, f32[128,384]{1,0:T(8,128)} %r_hbm.1, f32[2048,384]{1,0:T(8,128)} %t_hbm.1, ...), custom_call_target="tpu_custom_call" | custom-call | tf_op jit(solution)/shard_map/panel_step/pallas_call | solution.py:373
  67.3 0.8 %copy.16 = f32[2048,64]{0,1:T(8,128)} copy(f32[2048,64]{0,1:T(8,128)S(1)} %bitcast.6) | data formatting | bytes 1048576
  68.1 1.7 %copy.17 = f32[2048,384]{1,0:T(8,128)} copy(f32[2048,384]{1,0:T(8,128)S(1)} %get-tuple-element.17) | data formatting | bytes 6291456
  69.8 0.7 copy.18
  70.5 0.6 copy.19

commit v3 on v2

--- a/solution.py
+++ b/solution.py
@@ -33,24 +33,26 @@
     return lax.broadcasted_iota(jnp.int32, shape, dim)
 
 
-def invert_base(a):
-    n = a.shape[0]
+def invert_bases(blocks):
+    n = blocks[0].shape[0]
     i, j = iota((n, n), 0), iota((n, n), 1)
     eye = i == j
-    d = jnp.where(eye, a, 0.0)
-    inv_col = 1.0 / jnp.sum(d, axis=1, keepdims=True)
-    inv_row = 1.0 / jnp.sum(d, axis=0, keepdims=True)
-    inv = jnp.where(eye, inv_col, 0.0)
+    diag = [jnp.where(eye, a, 0.0) for a in blocks]
+    cols = [1.0 / jnp.sum(d, axis=1, keepdims=True) for d in diag]
+    rows = [1.0 / jnp.sum(d, axis=0, keepdims=True) for d in diag]
+    invs = [jnp.where(eye, col, 0.0) for col in cols]
     step = 1
     while step < n:
         pair = (i // (2 * step) == j // (2 * step)) & (i // step < j // step)
-        part = jnp.where(pair, a, 0.0)
+        parts = [jnp.where(pair, a, 0.0) for a in blocks]
         if step == 1:
-            inv = inv - part * inv_col * inv_row
+            invs = [inv - part * col * row for inv, part, col, row in zip(invs, parts, cols, rows)]
         else:
-            inv = inv - dot_high(dot_high(inv, part), inv)
+            mids = [dot_high(inv, part) for inv, part in zip(invs, parts)]
+            ends = [dot_high(mid, inv) for mid, inv in zip(mids, invs)]
+            invs = [inv - end for inv, end in zip(invs, ends)]
         step *= 2
-    return inv
+    return invs
 
 
 class Gather:
@@ -157,8 +159,8 @@
     nz, side, dt_hbm, gt_hbm, p_hbm, r_hbm, t_hbm, dg_hbm, rg_hbm, tg_hbm,
     pa_hbm, to_hbm, ro_hbm, do_hbm,
     dbuf, gbuf, rbuf, tbuf, pbuf, dgbuf, rgbuf, tgbuf, pabuf, dobuf,
-    aup, inv_t, tp_hi, tp_lo, g_hi, g_lo, wbuf, ubuf, rsbuf,
-    d_sems, g_sems, zs, zr, rs_s, rs_r, us, ur, local, outs,
+    aup, inv_t, tp_hi, tp_lo, g_hi, g_lo, wbuf, ubuf, vbuf, rsbuf, rvbuf,
+    d_sems, g_sems, zs, zr, rs_s, rs_r, us, ur, vs, vr, local, outs,
 ):
     z = lax.axis_index("row")
     c = lax.axis_index("col")
@@ -218,9 +220,6 @@
     dgat.start_first()
     dgat.start_own()
 
-    for load in loads[1:]:
-        load.wait()
-
     tile = 256
 
     def widen(i, carry):
@@ -234,29 +233,14 @@
         tp_lo[rows, k:] = lo
         return carry
 
+    for load in loads[1:3]:
+        load.wait()
+    lax.fori_loop(0, m // tile, widen, 0)
     dgat.relay()
     ggat.start_own()
     ggat.relay()
-    lax.fori_loop(0, m // tile, widen, 0)
-
     dgat.pass_own()
     dgat.pass_relayed()
-    for dy in range(side):
-        for dx in range(side):
-            dgat.wait_chip(dy, dx)
-    for col in range(ncol):
-        aup[col * w:(col + 1) * w, :] = jnp.concatenate([dbuf[col, i] for i in range(nz)], axis=1)
-
-    base = 128
-    inv_t[...] = jnp.zeros((n, n), F32)
-    for b in range(0, n, base):
-        inv_t[b:b + base, b:b + base] = invert_base(aup[b:b + base, b:b + base])
-    step = base
-    while step < n:
-        for b in range(0, n, 2 * step):
-            up, low = slice(b, b + step), slice(b + step, b + 2 * step)
-            inv_t[up, low] = -dot_high(dot_high(inv_t[up, up], aup[up, low]), inv_t[low, low])
-        step *= 2
 
     def take(dy, dx):
         at = ggat.col(-dy, -dx, 0)
@@ -266,9 +250,30 @@
         g_lo[rows, :] = value[1]
         wbuf[rows, :] = dot3(value, (tp_hi[...], tp_lo[...]))
 
-    ggat.pass_own()
+    for load in loads[3:]:
+        load.wait()
     ggat.wait_chip(0, 0)
     take(0, 0)
+    for dy in range(side):
+        for dx in range(side):
+            dgat.wait_chip(dy, dx)
+    for col in range(ncol):
+        aup[col * w:(col + 1) * w, :] = jnp.concatenate([dbuf[col, i] for i in range(nz)], axis=1)
+
+    base = 128
+    inv_t[...] = jnp.zeros((n, n), F32)
+    starts = range(0, n, base)
+    bases = invert_bases([aup[b:b + base, b:b + base] for b in starts])
+    for b, inv in zip(starts, bases):
+        inv_t[b:b + base, b:b + base] = inv
+    ggat.pass_own()
+    step = base
+    while step < n:
+        for b in range(0, n, 2 * step):
+            up, low = slice(b, b + step), slice(b + step, b + 2 * step)
+            inv_t[up, low] = -dot_high(dot_high(inv_t[up, up], aup[up, low]), inv_t[low, low])
+        step *= 2
+
     for i in range(1, side):
         ggat.wait_chip(0, i)
         take(0, i)
@@ -282,16 +287,28 @@
 
     wide_terms = split(wbuf[...])
     u_z = []
-    for i in range(1, nz):
+
+    def terms(i):
         to = lax.rem(z + i, nz)
         rows = pl.ds(pl.multiple_of(to * h, h), h)
-        ubuf[rows, :] = dot3(split(inv_t[rows, :]), wide_terms)
-        u_z.append(along_z(ubuf.at[rows], rsbuf.at[i], us, ur, i))
-        if i > 1:
-            u_z[i - 2].start()
-    rows = pl.ds(pl.multiple_of(z * h, h), h)
-    ubuf[rows, :] = dot3(split(inv_t[rows, :]), wide_terms)
-    u_z[-1].start()
+        value = dot3(split(inv_t[rows, :]), wide_terms)
+        ubuf[i] = value[:, :k]
+        vbuf[i] = value[:, k:k + w].T
+
+    order = sorted(range(1, nz), key=lambda i: -min(i, nz - i))
+    for at, i in enumerate(order):
+        terms(i)
+        u_z.append((
+            along_z(ubuf.at[i], rsbuf.at[i], us, ur, i),
+            along_z(vbuf.at[i], rvbuf.at[i], vs, vr, i),
+        ))
+        if at > 0:
+            for copy in u_z[at - 1]:
+                copy.start()
+    terms(0)
+    for copy in u_z[-1]:
+        copy.start()
+    u_z = [copy for pair in u_z for copy in pair]
 
     for copy in r_z:
         copy.wait_recv()
@@ -323,12 +340,13 @@
 
     for copy in u_z:
         copy.wait_recv()
-    total = ubuf[rows, :]
+    row_sum, diag_sum = ubuf[0], vbuf[0]
     for i in range(1, nz):
-        total = total + rsbuf[i]
-    rgbuf[...] = rgbuf[...] - total[:, :k]
+        row_sum = row_sum + rsbuf[i]
+        diag_sum = diag_sum + rvbuf[i]
+    rgbuf[...] = rgbuf[...] - row_sum
     keep = iota((w, h), 1) + z * h >= iota((w, h), 0) + c * w
-    dobuf[...] = jnp.where(keep, dgbuf[...] - total[:, k:k + w].T, 0.0)
+    dobuf[...] = jnp.where(keep, dgbuf[...] - diag_sum, 0.0)
     last = [
         pltpu.make_async_copy(rgbuf, ro_hbm, local.at[0]),
         pltpu.make_async_copy(dobuf, do_hbm, local.at[1]),
@@ -382,9 +400,10 @@
             vmem((n, n), F32), vmem((n, n), F32),
             vmem((m, wide), BF16), vmem((m, wide), BF16),
             vmem((n, m), BF16), vmem((n, m), BF16),
-            vmem((n, wide), F32), vmem((n, wide), F32), vmem((nz, h, wide), F32),
+            vmem((n, wide), F32), vmem((nz, h, k), F32), vmem((nz, w, h), F32),
+            vmem((nz, h, k), F32), vmem((nz, w, h), F32),
             gather_sems, list(gather_sems),
-            dma((nz,)), dma((nz,)), dma((nz,)), dma((nz,)), dma((nz,)), dma((nz,)),
+            *[dma((nz,)) for _ in range(8)],
             dma((8,)), dma((2, m // 256)),
         ],
         compiler_params=pltpu.CompilerParams(

time: 71.2 us -> 61.7 us (0.87)
  the two profiles are of different devices: /device:TPU:25 before, /device:TPU:16 now
where the time goes in v3:
time: 61.7 us; the launch traced here: 61.6 us
  Pallas kernels  57.2 us (93%)
  local copies, waits for them, and re-layouts  3.75 us (6%)
  between operations  0.64 us (1%)
    pallas_call x1, Pallas kernels, on_device(): pl.pallas_call(functools.partial(kernel, nz, side), out_shape=(shape((w,...  57.2 us
    unnamed x4, local copies, waits for them, and re-layouts  3.75 us

profile of v3, /device:TPU:16, one launch (start us, length us, event | category | flops | bytes accessed | tf_op | source)
XLA Modules:
  0.0 61.6 jit_solution(290190164134402581)
XLA Ops:
  0.6 57.2 %panel_step.1 = (f32[64,2048]{1,0:T(8,128)S(1)}, f32[2048,384]{1,0:T(8,128)S(1)}, f32[128,384]{1,0:T(8,128)S(1)}, f32[64,128]{1,0:T(8,128)S(1)}) custom-call(f32[64,128]{1,0:T(8,128)} %bitcast.10, f32[64,2048]{1,0:T(8,128)} %bitcast.8, f32[64,2048]{1,0:T(8,128)} %bitcast.9, f32[128,384]{1,0:T(8,128)} %r_hbm.1, f32[2048,384]{1,0:T(8,128)} %t_hbm.1, ...), custom_call_target="tpu_custom_call" | custom-call | tf_op jit(solution)/shard_map/panel_step/pallas_call | solution.py:391
  57.8 0.8 %copy.16 = f32[2048,64]{0,1:T(8,128)} copy(f32[2048,64]{0,1:T(8,128)S(1)} %bitcast.6) | data formatting | bytes 1048576
  58.6 1.7 %copy.17 = f32[2048,384]{1,0:T(8,128)} copy(f32[2048,384]{1,0:T(8,128)S(1)} %get-tuple-element.17) | data formatting | bytes 6291456
  60.3 0.7 %copy.18 = f32[128,384]{1,0:T(8,128)} copy(f32[128,384]{1,0:T(8,128)S(1)} %get-tuple-element.18) | data formatting | bytes 393216
  60.9 0.6 copy.19

commit v4 on v3

--- a/solution.py
+++ b/solution.py
@@ -288,27 +288,58 @@
     wide_terms = split(wbuf[...])
     u_z = []
 
-    def terms(i):
-        to = lax.rem(z + i, nz)
+    def terms(i, to):
         rows = pl.ds(pl.multiple_of(to * h, h), h)
         value = dot3(split(inv_t[rows, :]), wide_terms)
         ubuf[i] = value[:, :k]
         vbuf[i] = value[:, k:k + w].T
 
-    order = sorted(range(1, nz), key=lambda i: -min(i, nz - i))
-    for at, i in enumerate(order):
-        terms(i)
-        u_z.append((
-            along_z(ubuf.at[i], rsbuf.at[i], us, ur, i),
-            along_z(vbuf.at[i], rvbuf.at[i], vs, vr, i),
-        ))
-        if at > 0:
-            for copy in u_z[at - 1]:
+    def to_row(i, slot, to):
+        return [
+            pltpu.make_async_remote_copy(
+                src_ref=src.at[i], dst_ref=dst.at[slot], send_sem=send.at[i], recv_sem=recv.at[slot],
+                device_id=(to, c), device_id_type=MESH,
+            )
+            for src, dst, send, recv in ((ubuf, rsbuf, us, ur), (vbuf, rvbuf, vs, vr))
+        ]
+
+    joined = nz == 4
+    if joined:
+        end = (z == 0) | (z == nz - 1)
+        low = z < 2
+        partner = z + 1 - 2 * lax.rem(z, 2)
+        middle, far = jnp.where(low, 2, 1), jnp.where(low, nz - 1, 0)
+        near_z = to_row(1, 1, partner)
+        middle_z = to_row(2, jnp.where(end, 2, 3), middle)
+        far_z = to_row(3, jnp.where(end, 0, 2), jnp.where(end, partner, far))
+        terms(3, far)
+        terms(2, middle)
+
+        @pl.when(end)
+        def _():
+            for copy in far_z:
                 copy.start()
-    terms(0)
-    for copy in u_z[-1]:
-        copy.start()
-    u_z = [copy for pair in u_z for copy in pair]
+
+        terms(1, partner)
+        for copy in middle_z:
+            copy.start()
+        terms(0, z)
+        for copy in near_z:
+            copy.start()
+        u_z = near_z + middle_z + far_z
+    else:
+        order = sorted(range(1, nz), key=lambda i: -min(i, nz - i))
+        for at, i in enumerate(order):
+            to = lax.rem(z + i, nz)
+            terms(i, to)
+            u_z.append(to_row(i, i, to))
+            if at > 0:
+                for copy in u_z[at - 1]:
+                    copy.start()
+        terms(0, z)
+        for copy in u_z[-1]:
+            copy.start()
+        u_z = [copy for pair in u_z for copy in pair]
 
     for copy in r_z:
         copy.wait_recv()
@@ -326,6 +357,16 @@
 
     tp_hi[:n, :] = both[0]
     tp_lo[:n, :] = both[1]
+
+    if joined:
+        @pl.when(jnp.logical_not(end))
+        def _():
+            for copy in to_row(3, 0, partner):
+                copy.wait_recv()
+            ubuf[3] = ubuf[3] + rsbuf[0]
+            vbuf[3] = vbuf[3] + rvbuf[0]
+            for copy in far_z:
+                copy.start()
 
     def trail(i, carry):
         rows = pl.ds(pl.multiple_of(i * tile, tile), tile)
@@ -338,10 +379,21 @@
 
     lax.fori_loop(0, m // tile, trail, 0)
 
-    for copy in u_z:
-        copy.wait_recv()
+    if joined:
+        @pl.when(jnp.logical_not(end))
+        def _():
+            for copy in to_row(3, 3, partner):
+                copy.wait_recv()
+            ubuf[0] = ubuf[0] + rsbuf[3]
+            vbuf[0] = vbuf[0] + rvbuf[3]
+
+        for copy in to_row(1, 1, partner) + to_row(2, 2, partner):
+            copy.wait_recv()
+    else:
+        for copy in u_z:
+            copy.wait_recv()
     row_sum, diag_sum = ubuf[0], vbuf[0]
-    for i in range(1, nz):
+    for i in range(1, 3 if joined else nz):
         row_sum = row_sum + rsbuf[i]
         diag_sum = diag_sum + rvbuf[i]
     rgbuf[...] = rgbuf[...] - row_sum

time: 61.7 us -> 57.4 us (0.930)
  the two profiles are of different devices: /device:TPU:16 before, /device:TPU:25 now
where the time goes in v4:
time: 57.4 us; the launch traced here: 57.2 us
  Pallas kernels  52.8 us (92%)
  local copies, waits for them, and re-layouts  3.75 us (7%)
  between operations  0.64 us (1%)
    pallas_call x1, Pallas kernels, on_device(): pl.pallas_call(functools.partial(kernel, nz, side), out_shape=(shape((w,...  52.8 us
    unnamed x4, local copies, waits for them, and re-layouts  3.75 us

profile of v4, /device:TPU:25, one launch (start us, length us, event | category | flops | bytes accessed | tf_op | source)
XLA Modules:
  0.0 57.2 jit_solution(12237346374027645629)
XLA Ops:
  0.6 52.8 %panel_step.1 = (f32[64,2048]{1,0:T(8,128)S(1)}, f32[2048,384]{1,0:T(8,128)S(1)}, f32[128,384]{1,0:T(8,128)S(1)}, f32[64,128]{1,0:T(8,128)S(1)}) custom-call(f32[64,128]{1,0:T(8,128)} %bitcast.10, f32[64,2048]{1,0:T(8,128)} %bitcast.8, f32[64,2048]{1,0:T(8,128)} %bitcast.9, f32[128,384]{1,0:T(8,128)} %r_hbm.1, f32[2048,384]{1,0:T(8,128)} %t_hbm.1, ...), custom_call_target="tpu_custom_call" | custom-call | tf_op jit(solution)/shard_map/panel_step/pallas_call | solution.py:443
  53.4 0.8 %copy.16 = f32[2048,64]{0,1:T(8,128)} copy(f32[2048,64]{0,1:T(8,128)S(1)} %bitcast.6) | data formatting | bytes 1048576
  54.2 1.7 %copy.17 = f32[2048,384]{1,0:T(8,128)} copy(f32[2048,384]{1,0:T(8,128)S(1)} %get-tuple-element.17) | data formatting | bytes 6291456
  55.9 0.7 %copy.18 = f32[128,384]{1,0:T(8,128)} copy(f32[128,384]{1,0:T(8,128)S(1)} %get-tuple-element.18) | data formatting | bytes 393216
  56.5 0.6 %copy.19 = f32[128,64]{0,1:T(8,128)} copy(f32[128,64]{0,1:T(8,128)S(1)} %bitcast.7) | data formatting | bytes 65536
